TPU v7x, 256 devices: a whole 4x4x8 slice. The times are simulated.
256 devices in a mesh: grp: 32 (over x_hi, z, core), rep: 8 (over x_lo, y).
Axes of the slice: x: 4 (x_hi: 2, x_lo: 2; x = x_hi * 2 + x_lo), y: 4, z: 8, core: 2. Of those that a mesh axis runs over, the one named last changes fastest.
Arguments:
- features: bfloat16 [24576, 512], P(('grp', 'rep')), may hold values from -6 to 6
- tile_values: bfloat16 [768, 32, 2, 128, 128], P(('grp', 'rep')), may hold values from 0.019897461 to 1
- tile_columns: int32 [768, 32, 2], P(('grp', 'rep')), may hold values from 0 to 5, as said below
- tile_counts: int32 [768, 32], P(('grp', 'rep')), may hold values from 0 to 2
- state_ids: int32 [98304], P(('grp', 'rep')), may hold values from 0 to 24575
- self_weight: bfloat16 [512, 512], replicated, may hold values from -0.25 to 0.25
- neighbour_weight: bfloat16 [512, 512], replicated, may hold values from -0.25 to 0.25
- bias_vector: float32 [512], replicated, may hold values from -3 to 3
Outputs:
- embedded: bfloat16 [98304, 512], P(('grp', 'rep'))
Inputs may be any that keep to these rules, and one draw needn't show every extreme that they name: `tile_columns`: for each row block and group the first tile_counts entries name distinct column blocks of that group; entries beyond the count are padding and are ignored.
All inputs are finite; a program needn't handle non-finite values.
Results may differ from a plain program's by a relative error of at most 0.0033.
Values may be sent and summed in bfloat16 or wider, within the bound.
A program may use at most 192 MiB of HBM per device.

v0:
```python
import jax
import jax.numpy as jnp
from jax import lax
from jax.sharding import PartitionSpec as P


def on_device(
    features,
    tile_values,
    tile_columns,
    tile_counts,
    state_ids,
    self_weight,
    neighbour_weight,
    bias_vector,
):
    panels = lax.all_gather(features, "rep", axis=0, tiled=True)
    row_blocks = tile_values.shape[0]
    group_count = tile_values.shape[1]
    slot_count = tile_values.shape[2]
    tile_size = tile_values.shape[3]
    panel_rows = panels.shape[0]
    width = panels.shape[1]
    panel_blocks = panel_rows // tile_size
    local_rows = row_blocks * tile_size
    positions = lax.broadcasted_iota(jnp.int32, (row_blocks, group_count, slot_count), 2)
    usable = positions < tile_counts[:, :, None]
    row_sums = jnp.sum(tile_values, axis=4, dtype=jnp.float32)
    degree = 1.0 + jnp.sum(
        jnp.where(usable[:, :, :, None], row_sums, jnp.float32(0.0)), axis=(1, 2)
    ).reshape(local_rows)
    masked_values = jnp.where(usable[:, :, :, None, None], tile_values, jnp.zeros((), jnp.bfloat16))
    block_iota = lax.broadcasted_iota(jnp.int32, (1, 1, panel_blocks), 2)
    zero_value = jnp.zeros((), jnp.bfloat16)

    def dense_group(group):
        columns = lax.dynamic_index_in_dim(tile_columns, group, 1, keepdims=False)
        values = lax.dynamic_index_in_dim(masked_values, group, 1, keepdims=False)
        hits = columns[:, :, None] == block_iota
        dense = jnp.zeros((row_blocks, tile_size, panel_blocks, tile_size), jnp.bfloat16)
        for slot in range(slot_count):
            placed = jnp.where(
                hits[:, slot, None, :, None], values[:, slot, :, None, :], zero_value
            )
            dense = dense + placed
        return dense.reshape(local_rows, panel_rows)

    def group_product(window, group, totals):
        dense = dense_group(group)
        return totals + jnp.dot(dense, window, preferred_element_type=jnp.float32)

    everything = lax.all_gather(panels, "grp", axis=0, tiled=True)

    def each_group(group, running):
        window = lax.dynamic_slice_in_dim(everything, group * panel_rows, panel_rows, 0)
        return group_product(window, group, running)

    totals = lax.fori_loop(0, group_count, each_group, jnp.zeros((local_rows, width), jnp.float32))
    own_rows = jnp.take(everything, state_ids, axis=0)
    neighbour = (totals / jnp.sqrt(degree)[:, None]).astype(jnp.bfloat16)
    activation = jnp.dot(own_rows, self_weight, preferred_element_type=jnp.float32)
    activation = activation + jnp.dot(
        neighbour, neighbour_weight, preferred_element_type=jnp.float32
    )
    activation = activation + bias_vector[None, :]
    return jnp.maximum(activation, 0.0).astype(jnp.bfloat16)


def solution(mesh):
    placed = (
        P(("grp", "rep"), None),
        P(("grp", "rep"), None, None, None, None),
        P(("grp", "rep"), None, None),
        P(("grp", "rep"), None),
        P(("grp", "rep")),
        P(),
        P(),
        P(),
    )
    return jax.shard_map(
        on_device, mesh=mesh, in_specs=placed, out_specs=P(("grp", "rep"), None), check_vma=False
    )
```

profile of v0, /device:TPU:1, one launch (start us, length us, event | category | flops | bytes accessed | tf_op | source)
XLA Modules:
  0.0 342.0 jit_solution(12657822559184209282)
XLA Ops:
  6.5 27.6 %all_gather.6 = bf16[768,512]{1,0:T(8,128)(2,1)} all-gather(bf16[96,512]{1,0:T(8,128)(2,1)} %param.10), channel_id=1, replica_groups=mesh['grp'=32,'rep'=8] {'rep'}, dimensions={0}, use_global_device_ids=true | all-gather | bytes 884736 | tf_op jit(solution)/shard_map/all_gather | solution.py:17
  36.9 4.7 %convert_reduce_fusion = f32[3,32,2,128]{3,2,1,0:T(2,128)S(1)} fusion(bf16[3,32,2,128,128]{4,3,2,1,0:T(8,128)(2,1)} %param.11), kind=kLoop, calls=%fused_computation.15 | loop fusion | flops 6266880 | bytes 6389760 | tf_op jit(solution)/shard_map/reduce_sum | solution.py:28
  41.9 3.1 copy_select_fusion
  44.9 178.6 %all-gather.2.cloned.1.call-done = bf16[24576,512]{1,0:T(8,128)(2,1)} async-done(((bf16[768,512]{1,0:T(8,128)(2,1)}), bf16[24576,512]{1,0:T(8,128)(2,1)}) %all-gather.2.cloned.1.call-update) | async-done | bytes 25165840 | tf_op jit(solution)/shard_map/all_gather | solution.py:52
  223.6 96.5 %while.14 = (s32[]{:T(128)}, f32[384,512]{1,0:T(8,128)S(1)}, s32[3,32,2]{0,2,1:T(2,128)S(1)}, bf16[3,32,2,128,128]{4,3,0,2,1:T(8,128)(2,1)}, bf16[24576,512]{1,0...) while((s32[]{:T(128)}, f32[384,512]{1,0:T(8,128)S(1)}, ...), condition=%wide.region_1.2_spmd.clone, body=%wide.region_0.0_spmd.clone.sunk | while | flops 303267872 | bytes 4522361 | solution.py:58
  223.6 1.0 dynamic-slice_bitcast_fusion.5
  224.9 1.7 convolution_add_fusion.3
  226.6 0.9 dynamic-slice_bitcast_fusion.5
  227.9 1.7 convolution_add_fusion.3
  229.6 0.9 dynamic-slice_bitcast_fusion.5
  231.0 1.7 convolution_add_fusion.3
  234.0 1.7 convolution_add_fusion.3
  237.0 1.7 convolution_add_fusion.3
  240.0 1.7 convolution_add_fusion.3
  241.7 0.9 dynamic-slice_bitcast_fusion.5
  243.0 1.7 convolution_add_fusion.3
  246.0 1.7 convolution_add_fusion.3
  249.1 1.7 convolution_add_fusion.3
  250.7 0.9 dynamic-slice_bitcast_fusion.5
  252.1 1.7 convolution_add_fusion.3
  255.1 1.7 convolution_add_fusion.3
  256.8 0.9 dynamic-slice_bitcast_fusion.5
  258.1 1.7 convolution_add_fusion.3
  261.1 1.7 convolution_add_fusion.3
  262.8 0.9 dynamic-slice_bitcast_fusion.5
  264.1 1.7 convolution_add_fusion.3
  267.1 1.7 convolution_add_fusion.3
  270.2 1.7 convolution_add_fusion.3
  271.8 0.9 dynamic-slice_bitcast_fusion.5
  273.2 1.7 convolution_add_fusion.3
  276.2 1.7 convolution_add_fusion.3
  277.9 0.9 dynamic-slice_bitcast_fusion.5
  279.2 1.7 convolution_add_fusion.3
  282.2 1.7 convolution_add_fusion.3
  285.2 1.7 convolution_add_fusion.3
  288.2 1.7 convolution_add_fusion.3
  291.3 1.7 convolution_add_fusion.3
  294.3 1.7 convolution_add_fusion.3
  297.3 1.7 convolution_add_fusion.3
  300.3 1.7 convolution_add_fusion.3
  303.3 1.7 convolution_add_fusion.3
  306.3 1.7 convolution_add_fusion.3
  309.3 1.7 convolution_add_fusion.3
  312.4 1.7 convolution_add_fusion.3
  315.4 1.7 convolution_add_fusion.3
  318.4 1.7 convolution_add_fusion.3
  320.1 13.5 %gather_fusion = bf16[384,512]{1,0:T(8,128)(2,1)S(1)} fusion(bf16[24576,512]{1,0:T(8,128)(2,1)} %get-tuple-element.239, s32[1024]{0:T(1024)S(1)} %pad_clamp_fusion), kind=kCustom, calls=%fused_computation | custom fusion | bytes 787968 | tf_op jit(solution)/shard_map/jit(_take)/gather | solution.py:59
  334.0 1.2 fusion.8
  (205 shorter events, 36.1 us)
Async XLA Ops:
  6.5 327.0 %copy-start = (bf16[512,512]{1,0:T(8,128)(2,1)S(1)}, bf16[512,512]{1,0:T(8,128)(2,1)}, u32[]{:S(2)}) copy-start(bf16[512,512]{1,0:T(8,128)(2,1)} %param.15) | copy-start | bytes 1572868
  6.5 35.3 %copy-start.2 = (s32[384]{0:T(512)S(1)}, s32[384]{0:T(512)}, u32[]{:S(2)}) copy-start(s32[384]{0:T(512)} %param.14) | copy-start | bytes 4612
  6.5 217.0 %all-gather.2.cloned.1.call-start = ((), (), s32[]{:S(2)}) async-start(), calls=%async_computation | async-start | bytes 25952256 | tf_op jit(solution)/shard_map/all_gather | solution.py:52
  36.1 5.8 %copy-start.1 = (bf16[3,32,2,128,128]{4,3,2,1,0:T(8,128)(2,1)S(1)}, bf16[3,32,2,128,128]{4,3,2,1,0:T(8,128)(2,1)}, u32[]{:S(2)}) copy-start(bf16[3,32,2,128,128]{4,3,2,1,0:T(8,128)(2,1)} %param.11) | copy-start | bytes 18874372
  223.6 110.4 %copy-start.3 = (bf16[512,512]{1,0:T(8,128)(2,1)S(1)}, bf16[512,512]{1,0:T(8,128)(2,1)}, u32[]{:S(2)}) copy-start(bf16[512,512]{1,0:T(8,128)(2,1)} %param.16) | copy-start | bytes 1572868
  223.6 110.4 %copy-start.4 = (f32[512]{0:T(512)S(1)}, f32[512]{0:T(512)}, u32[]{:S(2)}) copy-start(f32[512]{0:T(512)} %param.17) | copy-start | bytes 6148
Sparse Core Ops, SparseCore 0:
  34.3 189.1 all-gather.1
where the time goes:
time: 344 us; the launch traced here: 342 us
  waiting for transfers between devices  179 us (52%)
  matrix products  54.9 us (16%)
  local copies, waits for them, and re-layouts  45.8 us (13%)
  blocking collectives  27.6 us (8%)
  other arithmetic  19.7 us (6%)
  between operations  13.5 us (4%)
    all_gather x1, waiting for transfers between devices, on_device(): everything = lax.all_gather(panels, 'grp', axis=0, tiled=True)  179 us
    dot_general x32, matrix products, group_product(): return totals + jnp.dot(dense, window, preferred_element_type=jnp.float32)  53.3 us
    squeeze x32, local copies, waits for them, and re-layouts, dense_group(): values = lax.dynamic_index_in_dim(masked_values, group, 1, keepdims=False)  30.3 us
    all_gather x1, blocking collectives, on_device(): panels = lax.all_gather(features, 'rep', axis=0, tiled=True)  27.6 us
    gather x1, local copies, waits for them, and re-layouts, on_device(): own_rows = jnp.take(everything, state_ids, axis=0)  13.5 us
    add x32, other arithmetic, dense_group(): dense = dense + placed  7.71 us
  transfers between devices with their start and end apart: 1, of which 1 were waited for; matrix products, arithmetic and copies ran while one was open for 3% of the time, Pallas kernels for 0%

commit v1 on v0

v1 whole, which is shorter than its diff:
```python
import jax
import jax.numpy as jnp
from jax import lax
from jax.sharding import PartitionSpec as P


def on_device(
    features,
    tile_values,
    tile_columns,
    tile_counts,
    state_ids,
    self_weight,
    neighbour_weight,
    bias_vector,
):
    panels = lax.all_gather(features, "rep", axis=0, tiled=True)
    everything = lax.all_gather(panels, "grp", axis=0, tiled=True)
    row_blocks, group_count, slot_count, tile_size, _ = tile_values.shape
    panel_rows = panels.shape[0]
    panel_blocks = panel_rows // tile_size
    local_rows = row_blocks * tile_size
    total_rows = everything.shape[0]

    positions = lax.broadcasted_iota(jnp.int32, (row_blocks, group_count, slot_count), 2)
    usable = positions < tile_counts[:, :, None]
    row_sums = jnp.sum(tile_values, axis=4, dtype=jnp.float32)
    degree = 1.0 + jnp.sum(
        jnp.where(usable[:, :, :, None], row_sums, jnp.float32(0.0)), axis=(1, 2)
    ).reshape(local_rows)

    block_iota = lax.broadcasted_iota(jnp.int32, (1, 1, 1, panel_blocks), 3)
    hits = (tile_columns[:, :, :, None] == block_iota) & usable[:, :, :, None]
    by_row = jnp.transpose(tile_values, (0, 3, 1, 2, 4))
    dense = jnp.zeros((row_blocks, tile_size, group_count, panel_blocks, tile_size), jnp.bfloat16)
    for slot in range(slot_count):
        dense = jnp.where(
            hits[:, None, :, slot, :, None], by_row[:, :, :, slot, None, :], dense
        )
    dense = dense.reshape(local_rows, total_rows)

    totals = jnp.dot(dense, everything, preferred_element_type=jnp.float32)
    own_rows = jnp.take(everything, state_ids, axis=0)
    neighbour = (totals / jnp.sqrt(degree)[:, None]).astype(jnp.bfloat16)
    activation = jnp.dot(own_rows, self_weight, preferred_element_type=jnp.float32)
    activation = activation + jnp.dot(
        neighbour, neighbour_weight, preferred_element_type=jnp.float32
    )
    activation = activation + bias_vector[None, :]
    return jnp.maximum(activation, 0.0).astype(jnp.bfloat16)


def solution(mesh):
    placed = (
        P(("grp", "rep"), None),
        P(("grp", "rep"), None, None, None, None),
        P(("grp", "rep"), None, None),
        P(("grp", "rep"), None),
        P(("grp", "rep")),
        P(),
        P(),
        P(),
    )
    return jax.shard_map(
        on_device, mesh=mesh, in_specs=placed, out_specs=P(("grp", "rep"), None), check_vma=False
    )
```

time: 344 us -> 267 us (0.78)
  waiting for transfers between devices: 179 us -> 131 us
  matrix products: 54.9 us -> 21.9 us
  local copies, waits for them, and re-layouts: 45.8 us -> 54.5 us
    all_gather x1, waiting for transfers between devices: 179 us -> 131 us  [on_device(): everything = lax.all_gather(panels, 'grp', axis=0, tiled=True)]
    dot_general x32 -> x1, matrix products: 53.3 us -> 20.3 us  [on_device(): totals = jnp.dot(dense, everything, preferred_element_type=jnp.float32)]
    select_n x0 -> x1, local copies, waits for them, and re-layouts: none -> 30.8 us  [on_device(): jnp.where(hits[:, None, :, slot, :, None], by_row[:, :, :, slot, None, :]...]
    squeeze x32 -> x0, local copies, waits for them, and re-layouts: 30.3 us -> none  [dense_group(): values = lax.dynamic_index_in_dim(masked_values, group, 1, keepdims=False)]
    broadcast_in_dim x64 -> x6, local copies, waits for them, and re-layouts: 0.66 us -> 10.1 us  [on_device(): jnp.where(hits[:, None, :, slot, :, None], by_row[:, :, :, slot, None, :]...]
    add x32 -> x0, other arithmetic: 7.71 us -> none  [dense_group(): dense = dense + placed]
    select_n x1, other arithmetic: 3.08 us -> 10.7 us  [on_device(): jnp.where(hits[:, None, :, slot, :, None], by_row[:, :, :, slot, None, :]...]
  transfers between devices with their start and end apart: 1 -> 1, of which waited for: 1 -> 1; matrix products, arithmetic and copies ran while one was open for 3% -> 22% of each run, Pallas kernels for 0% -> 0%
where the time goes in v1:
time: 267 us; the launch traced here: 266 us
  waiting for transfers between devices  131 us (49%)
  local copies, waits for them, and re-layouts  54.5 us (20%)
  blocking collectives  27.6 us (10%)
  matrix products  21.9 us (8%)
  other arithmetic  17 us (6%)
  between operations  13.5 us (5%)
    all_gather x1, waiting for transfers between devices, on_device(): everything = lax.all_gather(panels, 'grp', axis=0, tiled=True)  131 us
    select_n x1, local copies, waits for them, and re-layouts, on_device(): jnp.where(hits[:, None, :, slot, :, None], by_row[:, :, :, slot, None, :]...  30.8 us
    all_gather x1, blocking collectives, on_device(): panels = lax.all_gather(features, 'rep', axis=0, tiled=True)  27.6 us
    dot_general x1, matrix products, on_device(): totals = jnp.dot(dense, everything, preferred_element_type=jnp.float32)  20.3 us
    gather x1, local copies, waits for them, and re-layouts, on_device(): own_rows = jnp.take(everything, state_ids, axis=0)  13.5 us
    select_n x1, other arithmetic, on_device(): jnp.where(hits[:, None, :, slot, :, None], by_row[:, :, :, slot, None, :]...  10.7 us
    broadcast_in_dim x6, local copies, waits for them, and re-layouts, on_device(): jnp.where(hits[:, None, :, slot, :, None], by_row[:, :, :, slot, None, :]...  10.1 us
  transfers between devices with their start and end apart: 1, of which 1 were waited for; matrix products, arithmetic and copies ran while one was open for 22% of the time, Pallas kernels for 0%

profile of v1, /device:TPU:1, one launch (start us, length us, event | category | flops | bytes accessed | tf_op | source)
XLA Modules:
  0.0 265.8 jit_solution(17948136778856858964)
XLA Ops:
  6.5 0.0 copy-start
  6.5 0.0 all-gather.2.cloned.1.call-start
  6.5 27.6 %all_gather.6 = bf16[768,512]{1,0:T(8,128)(2,1)} all-gather(bf16[96,512]{1,0:T(8,128)(2,1)} %param.8), channel_id=1, replica_groups=mesh['grp'=32,'rep'=8] {'rep'}, dimensions={0}, use_global_device_ids=true | all-gather | bytes 884736 | tf_op jit(solution)/shard_map/all_gather | solution.py:17
  34.2 0.0 all-gather.2.cloned.1.call-update
  34.2 0.8 iota_compare_fusion
  35.0 0.1 copy.21
  35.1 0.7 fusion.8
  35.8 0.1 copy.22
  35.9 0.1 copy.24
  36.0 4.2 %slice_bitcast_fusion.1 = (bf16[3,128,32,128]{3,1,2,0:T(8,128)(2,1)S(1)}, bf16[3,128,32,128]{3,1,2,0:T(8,128)(2,1)S(1)}) fusion(bf16[3,128,32,2,128]{4,1,3,2,0:T(8,128)(2,1)} %bitcast.16), kind=kLoop, calls=%fused_computation.4 | loop fusion | bytes 12582912 | tf_op jit(solution)/shard_map/jit(_where)/broadcast_in_dim | solution.py:37
  40.2 2.0 copy.23
  42.3 3.6 %copy.25 = bf16[3,128,32,128]{3,2,1,0:T(8,128)(2,1)} copy(bf16[3,128,32,128]{3,1,2,0:T(8,128)(2,1)S(1)} %get-tuple-element.6) | data formatting | bytes 6291456 | tf_op jit(solution)/shard_map/jit(_where)/broadcast_in_dim | solution.py:37
  45.9 10.7 %select_select_fusion = bf16[3,128,32,6,128]{4,3,2,1,0:T(8,128)(2,1)} fusion(pred[3,32,6]{2,1,0:T(8,128)(4,1)S(1)} %copy.24, pred[3,32,6]{2,1,0:T(8,128)(4,1)S(1)} %copy.22, bf16[3,128,32,128]{3,2,1,0:T(8,128)(2,1)} %copy.25, bf16[3,128,32,128]{3,2,1,0:T(8,128)(2,1)S(1)} %copy.23), kind=kLoop, calls=%fused_computation.1 | loop fusion | flops 18874368 | bytes 25166976 | tf_op jit(solution)/shard_map/jit(_where)/select_n | solution.py:37
  56.7 0.0 copy-start.3
  56.7 30.8 %select_n.30 = bf16[384,24576]{1,0:T(8,128)(2,1)} reshape(bf16[3,128,32,6,128]{4,3,2,1,0:T(8,128)(2,1)} %select_select_fusion) | data formatting | bytes 37748736 | tf_op jit(solution)/shard_map/jit(_where)/select_n | solution.py:37
  87.5 0.0 copy-done.3
  87.5 4.6 %convert_reduce_fusion = f32[3,32,2,128]{3,2,1,0:T(2,128)S(1)} fusion(bf16[3,32,2,128,128]{4,3,2,1,0:T(8,128)(2,1)} %param.9), kind=kLoop, calls=%fused_computation.2 | loop fusion | flops 6266880 | bytes 6389760 | tf_op jit(solution)/shard_map/reduce_sum | solution.py:27
  92.1 0.2 select_reduce_fusion
  92.3 131.2 %all-gather.2.cloned.1.call-done = bf16[24576,512]{1,0:T(8,128)(2,1)} async-done(((bf16[768,512]{1,0:T(8,128)(2,1)}), bf16[24576,512]{1,0:T(8,128)(2,1)}) %all-gather.2.cloned.1.call-update) | async-done | bytes 25165840 | tf_op jit(solution)/shard_map/all_gather | solution.py:18
  223.6 13.5 %gather_fusion = bf16[384,512]{1,0:T(8,128)(2,1)S(1)} fusion(bf16[24576,512]{1,0:T(8,128)(2,1)} %all-gather.2.cloned.1.call-done, s32[1024]{0:T(1024)S(1)} %pad_clamp_fusion), kind=kCustom, calls=%fused_computation | custom fusion | bytes 787968 | tf_op jit(solution)/shard_map/jit(_take)/gather | solution.py:43
  237.0 0.0 copy-done
  237.0 0.4 fusion.4
  237.5 0.0 copy-start.2
  237.5 0.0 copy-start.4
  237.5 0.0 copy-start.1
  237.5 20.3 %fusion.3 = bf16[384,512]{1,0:T(8,128)(2,1)S(1)} fusion(bf16[384,24576]{1,0:T(8,128)(2,1)} %select_n.30, bf16[24576,512]{1,0:T(8,128)(2,1)} %all-gather.2.cloned.1.call-done, f32[384]{0:T(512)S(1)} %sqrt_bitcast_fusion), kind=kOutput, calls=%fused_computation.10 | convolution fusion | flops 9664069632 | bytes 44434944 | tf_op jit(solution)/shard_map/dot_general | solution.py:42
  257.8 0.0 copy-done.2
  257.8 0.0 copy-done.4
  257.9 1.1 fusion.2
  259.0 0.0 copy-done.1
  (5 shorter events, 0.0 us)
Async XLA Ops:
  6.5 230.5 %copy-start = (bf16[512,512]{1,0:T(8,128)(2,1)S(1)}, bf16[512,512]{1,0:T(8,128)(2,1)}, u32[]{:S(2)}) copy-start(bf16[512,512]{1,0:T(8,128)(2,1)} %param.13) | copy-start | bytes 1572868
  6.5 217.0 %all-gather.2.cloned.1.call-start = ((), (), s32[]{:S(2)}) async-start(), calls=%async_computation | async-start | bytes 25952256 | tf_op jit(solution)/shard_map/all_gather | solution.py:18
  56.7 30.8 %copy-start.3 = (s32[384]{0:T(512)S(1)}, s32[384]{0:T(512)}, u32[]{:S(2)}) copy-start(s32[384]{0:T(512)} %param.12) | copy-start | bytes 4612
  237.5 20.4 %copy-start.2 = (bf16[512,512]{1,0:T(8,128)(2,1)S(1)}, bf16[512,512]{1,0:T(8,128)(2,1)}, u32[]{:S(2)}) copy-start(bf16[512,512]{1,0:T(8,128)(2,1)} %param.14) | copy-start | bytes 1572868
  237.5 20.4 %copy-start.4 = (f32[512]{0:T(512)S(1)}, f32[512]{0:T(512)}, u32[]{:S(2)}) copy-start(f32[512]{0:T(512)} %param.15) | copy-start | bytes 6148
  237.5 21.5 %copy-start.1 = (bf16[512,512]{1,0:T(8,128)(2,1)S(1)}, bf16[512,512]{1,0:T(8,128)(2,1)}, u32[]{:S(2)}) copy-start(bf16[512,512]{1,0:T(8,128)(2,1)} %param.13) | copy-start | bytes 1572868
Sparse Core Ops, SparseCore 0:
  34.3 189.1 all-gather.1

commit v2 on v1

--- a/solution.py
+++ b/solution.py
@@ -1,7 +1,65 @@
+import functools
+
 import jax
 import jax.numpy as jnp
 from jax import lax
+from jax.experimental import pallas as pl
+from jax.experimental.pallas import tpu as pltpu
 from jax.sharding import PartitionSpec as P
+
+
+def rep_gather_kernel(count, x_ref, o_ref, send_sem, recv_sem):
+    me = lax.axis_index("rep")
+    team = lax.axis_index("grp")
+    rows = x_ref.shape[0]
+    mesh_id = pl.DeviceIdType.MESH
+    barrier = pltpu.get_barrier_semaphore()
+    for step in range(1, count):
+        peer = lax.rem(me + step, count)
+        pl.semaphore_signal(barrier, inc=1, device_id=(team, peer), device_id_type=mesh_id)
+    pl.semaphore_wait(barrier, count - 1)
+    sends = []
+    for step in range(1, count):
+        peer = lax.rem(me + step, count)
+        copy = pltpu.make_async_remote_copy(
+            src_ref=x_ref,
+            dst_ref=o_ref.at[pl.ds(pl.multiple_of(me * rows, rows), rows)],
+            send_sem=send_sem.at[step],
+            recv_sem=recv_sem.at[step],
+            device_id=(team, peer),
+            device_id_type=mesh_id,
+        )
+        copy.start()
+        sends.append(copy)
+    o_ref[pl.ds(pl.multiple_of(me * rows, rows), rows), :] = x_ref[...]
+    for step in range(1, count):
+        source = lax.rem(me + count - step, count)
+        arriving = pltpu.make_async_remote_copy(
+            src_ref=x_ref,
+            dst_ref=o_ref.at[pl.ds(pl.multiple_of(source * rows, rows), rows)],
+            send_sem=send_sem.at[step],
+            recv_sem=recv_sem.at[step],
+            device_id=(team, source),
+            device_id_type=mesh_id,
+        )
+        arriving.wait_recv()
+    for copy in sends:
+        copy.wait_send()
+
+
+def rep_gather(x, count):
+    rows, width = x.shape
+    return pl.pallas_call(
+        functools.partial(rep_gather_kernel, count),
+        out_shape=jax.ShapeDtypeStruct((rows * count, width), x.dtype),
+        in_specs=[pl.BlockSpec(memory_space=pltpu.VMEM)],
+        out_specs=pl.BlockSpec(memory_space=pltpu.VMEM),
+        scratch_shapes=[
+            pltpu.SemaphoreType.DMA((count,)),
+            pltpu.SemaphoreType.DMA((count,)),
+        ],
+        compiler_params=pltpu.CompilerParams(collective_id=0, has_side_effects=True),
+    )(x)
 
 
 def on_device(
@@ -14,7 +72,7 @@
     neighbour_weight,
     bias_vector,
 ):
-    panels = lax.all_gather(features, "rep", axis=0, tiled=True)
+    panels = rep_gather(features, REP_COUNT[0])
     everything = lax.all_gather(panels, "grp", axis=0, tiled=True)
     row_blocks, group_count, slot_count, tile_size, _ = tile_values.shape
     panel_rows = panels.shape[0]
@@ -50,7 +108,11 @@
     return jnp.maximum(activation, 0.0).astype(jnp.bfloat16)
 
 
+REP_COUNT = [8]
+
+
 def solution(mesh):
+    REP_COUNT[0] = mesh.shape["rep"]
     placed = (
         P(("grp", "rep"), None),
         P(("grp", "rep"), None, None, None, None),

time: 267 us -> 251 us (0.940)
  blocking collectives: 27.6 us -> 0 us
  Pallas kernels: 0 us -> 17 us
  waiting for transfers between devices: 131 us -> 126 us
    all_gather x1 -> x0, blocking collectives: 27.6 us -> none  [on_device(): panels = lax.all_gather(features, 'rep', axis=0, tiled=True)]
    pallas_call x0 -> x1, Pallas kernels: none -> 17 us  [rep_gather(): pl.pallas_call(functools.partial(rep_gather_kernel, count), out_shape=jax...]
    all_gather x1, waiting for transfers between devices: 131 us -> 126 us  [on_device(): everything = lax.all_gather(panels, 'grp', axis=0, tiled=True)]
  transfers between devices with their start and end apart: 1 -> 1, of which waited for: 1 -> 1; matrix products, arithmetic and copies ran while one was open for 22% -> 23% of each run, Pallas kernels for 0% -> 0%
where the time goes in v2:
time: 251 us; the launch traced here: 250 us
  waiting for transfers between devices  126 us (50%)
  local copies, waits for them, and re-layouts  54.5 us (22%)
  matrix products  21.9 us (9%)
  Pallas kernels  17 us (7%)
  other arithmetic  16.7 us (7%)
  between operations  13.5 us (5%)
    all_gather x1, waiting for transfers between devices, on_device(): everything = lax.all_gather(panels, 'grp', axis=0, tiled=True)  126 us
    select_n x1, local copies, waits for them, and re-layouts, on_device(): jnp.where(hits[:, None, :, slot, :, None], by_row[:, :, :, slot, None, :]...  30.8 us
    dot_general x1, matrix products, on_device(): totals = jnp.dot(dense, everything, preferred_element_type=jnp.float32)  20.3 us
    pallas_call x1, Pallas kernels, rep_gather(): pl.pallas_call(functools.partial(rep_gather_kernel, count), out_shape=jax...  17 us
    gather x1, local copies, waits for them, and re-layouts, on_device(): own_rows = jnp.take(everything, state_ids, axis=0)  13.5 us
    select_n x1, other arithmetic, on_device(): jnp.where(hits[:, None, :, slot, :, None], by_row[:, :, :, slot, None, :]...  10.4 us
    broadcast_in_dim x6, local copies, waits for them, and re-layouts, on_device(): jnp.where(hits[:, None, :, slot, :, None], by_row[:, :, :, slot, None, :]...  10.1 us
  transfers between devices with their start and end apart: 1, of which 1 were waited for; matrix products, arithmetic and copies ran while one was open for 23% of the time, Pallas kernels for 0%

profile of v2, /device:TPU:1, one launch (start us, length us, event | category | flops | bytes accessed | tf_op | source)
XLA Modules:
  0.0 250.0 jit_solution(4905550121301455053)
XLA Ops:
  6.5 0.0 copy-start
  6.5 0.0 all-gather.2.cloned.1.call-start
  6.5 17.0 %shard_map.82 = bf16[768,512]{1,0:T(8,128)(2,1)} custom-call(bf16[96,512]{1,0:T(8,128)(2,1)} %x_ref.1), custom_call_target="tpu_custom_call" | custom-call | tf_op jit(solution)/shard_map/pallas_call | solution.py:52
  23.5 0.0 all-gather.2.cloned.1.call-update
  23.6 0.8 iota_compare_fusion
  24.3 0.1 copy.21
  24.4 0.7 fusion.8
  25.1 0.1 copy.22
  25.3 0.1 copy.24
  25.4 4.2 %slice_bitcast_fusion.1 = (bf16[3,128,32,128]{3,1,2,0:T(8,128)(2,1)S(1)}, bf16[3,128,32,128]{3,1,2,0:T(8,128)(2,1)S(1)}) fusion(bf16[3,128,32,2,128]{4,1,3,2,0:T(8,128)(2,1)} %bitcast.16), kind=kLoop, calls=%fused_computation.4 | loop fusion | bytes 12582912 | tf_op jit(solution)/shard_map/jit(_where)/broadcast_in_dim | solution.py:95
  29.6 2.0 copy.23
  31.6 3.6 %copy.25 = bf16[3,128,32,128]{3,2,1,0:T(8,128)(2,1)} copy(bf16[3,128,32,128]{3,1,2,0:T(8,128)(2,1)S(1)} %get-tuple-element.6) | data formatting | bytes 6291456 | tf_op jit(solution)/shard_map/jit(_where)/broadcast_in_dim | solution.py:95
  35.3 10.4 %select_select_fusion = bf16[3,128,32,6,128]{4,3,2,1,0:T(8,128)(2,1)} fusion(pred[3,32,6]{2,1,0:T(8,128)(4,1)S(1)} %copy.24, pred[3,32,6]{2,1,0:T(8,128)(4,1)S(1)} %copy.22, bf16[3,128,32,128]{3,2,1,0:T(8,128)(2,1)} %copy.25, bf16[3,128,32,128]{3,2,1,0:T(8,128)(2,1)S(1)} %copy.23), kind=kLoop, calls=%fused_computation.1 | loop fusion | flops 18874368 | bytes 25166976 | tf_op jit(solution)/shard_map/jit(_where)/select_n | solution.py:95
  45.7 0.0 copy-start.3
  45.7 30.8 %select_n.30 = bf16[384,24576]{1,0:T(8,128)(2,1)} reshape(bf16[3,128,32,6,128]{4,3,2,1,0:T(8,128)(2,1)} %select_select_fusion) | data formatting | bytes 37748736 | tf_op jit(solution)/shard_map/jit(_where)/select_n | solution.py:95
  76.5 0.0 copy-done.3
  76.5 4.6 %convert_reduce_fusion = f32[3,32,2,128]{3,2,1,0:T(2,128)S(1)} fusion(bf16[3,32,2,128,128]{4,3,2,1,0:T(8,128)(2,1)} %param.9), kind=kLoop, calls=%fused_computation.2 | loop fusion | flops 6266880 | bytes 6389760 | tf_op jit(solution)/shard_map/reduce_sum | solution.py:85
  81.1 0.2 select_reduce_fusion
  81.3 126.4 %all-gather.2.cloned.1.call-done = bf16[24576,512]{1,0:T(8,128)(2,1)} async-done(((bf16[768,512]{1,0:T(8,128)(2,1)}), bf16[24576,512]{1,0:T(8,128)(2,1)}) %all-gather.2.cloned.1.call-update) | async-done | bytes 25165840 | tf_op jit(solution)/shard_map/all_gather | solution.py:76
  207.7 13.5 %gather_fusion = bf16[384,512]{1,0:T(8,128)(2,1)S(1)} fusion(bf16[24576,512]{1,0:T(8,128)(2,1)} %all-gather.2.cloned.1.call-done, s32[1024]{0:T(1024)S(1)} %pad_clamp_fusion), kind=kCustom, calls=%fused_computation | custom fusion | bytes 787968 | tf_op jit(solution)/shard_map/jit(_take)/gather | solution.py:101
  221.2 0.0 copy-done
  221.2 0.4 fusion.4
  221.6 0.0 copy-start.2
  221.6 0.0 copy-start.4
  221.6 0.0 copy-start.1
  221.7 20.3 %fusion.3 = bf16[384,512]{1,0:T(8,128)(2,1)S(1)} fusion(bf16[384,24576]{1,0:T(8,128)(2,1)} %select_n.30, bf16[24576,512]{1,0:T(8,128)(2,1)} %all-gather.2.cloned.1.call-done, f32[384]{0:T(512)S(1)} %sqrt_bitcast_fusion), kind=kOutput, calls=%fused_computation.10 | convolution fusion | flops 9664069632 | bytes 44434944 | tf_op jit(solution)/shard_map/dot_general | solution.py:100
  242.0 0.0 copy-done.2
  242.0 0.0 copy-done.4
  242.0 1.1 fusion.2
  243.1 0.0 copy-done.1
  (5 shorter events, 0.0 us)
Async XLA Ops:
  6.5 214.7 %copy-start = (bf16[512,512]{1,0:T(8,128)(2,1)S(1)}, bf16[512,512]{1,0:T(8,128)(2,1)}, u32[]{:S(2)}) copy-start(bf16[512,512]{1,0:T(8,128)(2,1)} %param.13) | copy-start | bytes 1572868
  6.5 201.2 %all-gather.2.cloned.1.call-start = ((), (), s32[]{:S(2)}) async-start(), calls=%async_computation | async-start | bytes 25952256 | tf_op jit(solution)/shard_map/all_gather | solution.py:76
  45.7 30.8 %copy-start.3 = (s32[384]{0:T(512)S(1)}, s32[384]{0:T(512)}, u32[]{:S(2)}) copy-start(s32[384]{0:T(512)} %param.12) | copy-start | bytes 4612
  221.6 20.4 %copy-start.2 = (bf16[512,512]{1,0:T(8,128)(2,1)S(1)}, bf16[512,512]{1,0:T(8,128)(2,1)}, u32[]{:S(2)}) copy-start(bf16[512,512]{1,0:T(8,128)(2,1)} %param.14) | copy-start | bytes 1572868
  221.6 20.4 %copy-start.4 = (f32[512]{0:T(512)S(1)}, f32[512]{0:T(512)}, u32[]{:S(2)}) copy-start(f32[512]{0:T(512)} %param.15) | copy-start | bytes 6148
  221.6 21.5 %copy-start.1 = (bf16[512,512]{1,0:T(8,128)(2,1)S(1)}, bf16[512,512]{1,0:T(8,128)(2,1)}, u32[]{:S(2)}) copy-start(bf16[512,512]{1,0:T(8,128)(2,1)} %param.13) | copy-start | bytes 1572868
Sparse Core Ops, SparseCore 0:
  23.7 183.9 all-gather.1

commit v3 on v2

--- a/solution.py
+++ b/solution.py
@@ -45,6 +45,38 @@
         arriving.wait_recv()
     for copy in sends:
         copy.wait_send()
+
+
+def row_gather_kernel(ids_ref, table_ref, out_ref, sem):
+    count = ids_ref.shape[0]
+    last = table_ref.shape[0] - 1
+
+    def issue(r, carry):
+        row = jnp.minimum(jnp.maximum(ids_ref[r], 0), last)
+        start = pl.multiple_of((row // 2) * 2, 2)
+        pltpu.make_async_copy(
+            table_ref.at[pl.ds(start, 2)], out_ref.at[pl.ds(pl.multiple_of(r * 2, 2), 2)], sem
+        ).start()
+        return carry
+
+    lax.fori_loop(0, count, issue, 0)
+    pltpu.make_async_copy(table_ref.at[pl.ds(0, 2 * count)], out_ref, sem).wait()
+
+
+def row_gather(table, ids):
+    count, width = ids.shape[0], table.shape[1]
+    pairs = pl.pallas_call(
+        row_gather_kernel,
+        out_shape=jax.ShapeDtypeStruct((2 * count, width), table.dtype),
+        in_specs=[
+            pl.BlockSpec(memory_space=pltpu.SMEM),
+            pl.BlockSpec(memory_space=pl.ANY),
+        ],
+        out_specs=pl.BlockSpec(memory_space=pltpu.VMEM),
+        scratch_shapes=[pltpu.SemaphoreType.DMA(())],
+    )(ids, table).reshape(count, 2, width)
+    odd = (ids % 2 == 1)[:, None]
+    return jnp.where(odd, pairs[:, 1, :], pairs[:, 0, :])
 
 
 def rep_gather(x, count):
@@ -98,7 +130,7 @@
     dense = dense.reshape(local_rows, total_rows)
 
     totals = jnp.dot(dense, everything, preferred_element_type=jnp.float32)
-    own_rows = jnp.take(everything, state_ids, axis=0)
+    own_rows = row_gather(everything, state_ids)
     neighbour = (totals / jnp.sqrt(degree)[:, None]).astype(jnp.bfloat16)
     activation = jnp.dot(own_rows, self_weight, preferred_element_type=jnp.float32)
     activation = activation + jnp.dot(

time: 251 us -> 249 us (level)
  local copies, waits for them, and re-layouts: 54.5 us -> 44.3 us
  Pallas kernels: 17 us -> 25.7 us
    gather x1 -> x0, local copies, waits for them, and re-layouts: 13.5 us -> none  [on_device(): own_rows = jnp.take(everything, state_ids, axis=0)]
    pallas_call x0 -> x1, Pallas kernels: none -> 8.76 us  [row_gather(): pl.pallas_call(row_gather_kernel, out_shape=jax.ShapeDtypeStruct((2 * cou...]
where the time goes in v3:
time: 249 us; the launch traced here: 248 us
  waiting for transfers between devices  126 us (51%)
  local copies, waits for them, and re-layouts  44.3 us (18%)
  Pallas kernels  25.7 us (10%)
  matrix products  21.6 us (9%)
  other arithmetic  16.7 us (7%)
  between operations  13.5 us (5%)
    all_gather x1, waiting for transfers between devices, on_device(): everything = lax.all_gather(panels, 'grp', axis=0, tiled=True)  126 us
    select_n x1, local copies, waits for them, and re-layouts, on_device(): jnp.where(hits[:, None, :, slot, :, None], by_row[:, :, :, slot, None, :]...  30.8 us
    dot_general x1, matrix products, on_device(): totals = jnp.dot(dense, everything, preferred_element_type=jnp.float32)  20.1 us
    pallas_call x1, Pallas kernels, rep_gather(): pl.pallas_call(functools.partial(rep_gather_kernel, count), out_shape=jax...  17 us
    select_n x1, other arithmetic, on_device(): jnp.where(hits[:, None, :, slot, :, None], by_row[:, :, :, slot, None, :]...  10.4 us
    broadcast_in_dim x6, local copies, waits for them, and re-layouts, on_device(): jnp.where(hits[:, None, :, slot, :, None], by_row[:, :, :, slot, None, :]...  10.1 us
    pallas_call x1, Pallas kernels, row_gather(): pl.pallas_call(row_gather_kernel, out_shape=jax.ShapeDtypeStruct((2 * cou...  8.76 us
  transfers between devices with their start and end apart: 1, of which 1 were waited for; matrix products, arithmetic and copies ran while one was open for 23% of the time, Pallas kernels for 0%

profile of v3, /device:TPU:1, one launch (start us, length us, event | category | flops | bytes accessed | tf_op | source)
XLA Modules:
  0.0 248.3 jit_solution(12579766729313486861)
XLA Ops:
  6.5 0.0 copy-start
  6.5 0.0 all-gather.2.cloned.1.call-start
  6.5 17.0 %shard_map.82 = bf16[768,512]{1,0:T(8,128)(2,1)} custom-call(bf16[96,512]{1,0:T(8,128)(2,1)} %x_ref.1), custom_call_target="tpu_custom_call" | custom-call | tf_op jit(solution)/shard_map/pallas_call | solution.py:84
  23.5 0.0 all-gather.2.cloned.1.call-update
  23.6 0.8 iota_compare_fusion
  24.3 0.1 copy.28
  24.4 0.7 fusion.8
  25.1 0.1 copy.29
  25.3 0.1 copy.31
  25.4 4.2 %slice_bitcast_fusion.1 = (bf16[3,128,32,128]{3,1,2,0:T(8,128)(2,1)S(1)}, bf16[3,128,32,128]{3,1,2,0:T(8,128)(2,1)S(1)}) fusion(bf16[3,128,32,2,128]{4,1,3,2,0:T(8,128)(2,1)} %bitcast.26), kind=kLoop, calls=%fused_computation.3 | loop fusion | bytes 12582912 | tf_op jit(solution)/shard_map/jit(_where)/broadcast_in_dim | solution.py:127
  29.6 2.0 copy.30
  31.6 3.6 %copy.32 = bf16[3,128,32,128]{3,2,1,0:T(8,128)(2,1)} copy(bf16[3,128,32,128]{3,1,2,0:T(8,128)(2,1)S(1)} %get-tuple-element.6) | data formatting | bytes 6291456 | tf_op jit(solution)/shard_map/jit(_where)/broadcast_in_dim | solution.py:127
  35.3 10.4 %select_select_fusion = bf16[3,128,32,6,128]{4,3,2,1,0:T(8,128)(2,1)} fusion(pred[3,32,6]{2,1,0:T(8,128)(4,1)S(1)} %copy.31, pred[3,32,6]{2,1,0:T(8,128)(4,1)S(1)} %copy.29, bf16[3,128,32,128]{3,2,1,0:T(8,128)(2,1)} %copy.32, bf16[3,128,32,128]{3,2,1,0:T(8,128)(2,1)S(1)} %copy.30), kind=kLoop, calls=%fused_computation | loop fusion | flops 18874368 | bytes 25166976 | tf_op jit(solution)/shard_map/jit(_where)/select_n | solution.py:127
  45.7 0.0 copy-start.2
  45.7 30.8 %select_n.32 = bf16[384,24576]{1,0:T(8,128)(2,1)} reshape(bf16[3,128,32,6,128]{4,3,2,1,0:T(8,128)(2,1)} %select_select_fusion) | data formatting | bytes 37748736 | tf_op jit(solution)/shard_map/jit(_where)/select_n | solution.py:127
  76.5 4.6 %convert_reduce_fusion = f32[3,32,2,128]{3,2,1,0:T(2,128)S(1)} fusion(bf16[3,32,2,128,128]{4,3,2,1,0:T(8,128)(2,1)} %param.9), kind=kLoop, calls=%fused_computation.1 | loop fusion | flops 6266880 | bytes 6389760 | tf_op jit(solution)/shard_map/reduce_sum | solution.py:117
  81.1 0.2 select_reduce_fusion
  81.3 0.0 copy-done.2
  81.3 126.4 %all-gather.2.cloned.1.call-done.table_ref = bf16[24576,512]{1,0:T(8,128)(2,1)} async-done(((bf16[768,512]{1,0:T(8,128)(2,1)}), bf16[24576,512]{1,0:T(8,128)(2,1)}) %all-gather.2.cloned.1.call-update) | async-done | bytes 25165840 | tf_op jit(solution)/shard_map/all_gather | solution.py:108
  207.7 8.8 %shard_map.83 = bf16[768,512]{1,0:T(8,128)(2,1)} custom-call(s32[384]{0:T(512)} %ids_ref.1, bf16[24576,512]{1,0:T(8,128)(2,1)} %all-gather.2.cloned.1.call-done.table_ref), custom_call_target="tpu_custom_call" | custom-call | tf_op jit(solution)/shard_map/pallas_call | solution.py:68
  216.5 2.2 reshape.31
  218.6 1.1 fusion.11
  219.7 0.0 copy-done
  219.7 0.4 fusion.5
  220.2 0.0 copy-start.1
  220.2 0.0 copy-start.3
  220.2 20.1 %fusion.3 = bf16[384,512]{1,0:T(8,128)(2,1)S(1)} fusion(bf16[384,24576]{1,0:T(8,128)(2,1)} %select_n.32, bf16[24576,512]{1,0:T(8,128)(2,1)} %all-gather.2.cloned.1.call-done.table_ref, f32[384]{0:T(512)S(1)} %sqrt_bitcast_fusion), kind=kOutput, calls=%fused_computation.9 | convolution fusion | flops 9664069632 | bytes 44434944 | tf_op jit(solution)/shard_map/dot_general | solution.py:132
  240.3 0.0 copy-done.1
  240.3 0.0 copy-done.3
  240.3 1.1 fusion.2
  (3 shorter events, 0.0 us)
Async XLA Ops:
  6.5 213.2 %copy-start = (bf16[512,512]{1,0:T(8,128)(2,1)S(1)}, bf16[512,512]{1,0:T(8,128)(2,1)}, u32[]{:S(2)}) copy-start(bf16[512,512]{1,0:T(8,128)(2,1)} %param.13) | copy-start | bytes 1572868
  6.5 201.2 %all-gather.2.cloned.1.call-start = ((), (), s32[]{:S(2)}) async-start(), calls=%async_computation | async-start | bytes 25952256 | tf_op jit(solution)/shard_map/all_gather | solution.py:108
  45.7 35.6 %copy-start.2 = (s32[384]{0:T(512)S(1)}, s32[384]{0:T(512)}, u32[]{:S(2)}) copy-start(s32[384]{0:T(512)} %ids_ref.1) | copy-start | bytes 4612
  220.2 20.1 %copy-start.1 = (bf16[512,512]{1,0:T(8,128)(2,1)S(1)}, bf16[512,512]{1,0:T(8,128)(2,1)}, u32[]{:S(2)}) copy-start(bf16[512,512]{1,0:T(8,128)(2,1)} %param.14) | copy-start | bytes 1572868
  220.2 20.1 %copy-start.3 = (f32[512]{0:T(512)S(1)}, f32[512]{0:T(512)}, u32[]{:S(2)}) copy-start(f32[512]{0:T(512)} %param.15) | copy-start | bytes 6148
Sparse Core Ops, SparseCore 0:
  23.7 183.9 all-gather.1

commit v4 on v3

--- a/solution.py
+++ b/solution.py
@@ -59,7 +59,7 @@
         ).start()
         return carry
 
-    lax.fori_loop(0, count, issue, 0)
+    lax.fori_loop(0, count, issue, 0, unroll=16)
     pltpu.make_async_copy(table_ref.at[pl.ds(0, 2 * count)], out_ref, sem).wait()
 
 

time: 249 us -> 248 us (level)
  no operation moved by 1% of the time
where the time goes in v4:
time: 248 us; the launch traced here: 247 us
  waiting for transfers between devices  126 us (51%)
  local copies, waits for them, and re-layouts  44.3 us (18%)
  Pallas kernels  24.1 us (10%)
  matrix products  21.6 us (9%)
  other arithmetic  16.7 us (7%)
  between operations  13.5 us (5%)
    all_gather x1, waiting for transfers between devices, on_device(): everything = lax.all_gather(panels, 'grp', axis=0, tiled=True)  126 us
    select_n x1, local copies, waits for them, and re-layouts, on_device(): jnp.where(hits[:, None, :, slot, :, None], by_row[:, :, :, slot, None, :]...  30.8 us
    dot_general x1, matrix products, on_device(): totals = jnp.dot(dense, everything, preferred_element_type=jnp.float32)  20.1 us
    pallas_call x1, Pallas kernels, rep_gather(): pl.pallas_call(functools.partial(rep_gather_kernel, count), out_shape=jax...  17 us
    select_n x1, other arithmetic, on_device(): jnp.where(hits[:, None, :, slot, :, None], by_row[:, :, :, slot, None, :]...  10.4 us
    broadcast_in_dim x6, local copies, waits for them, and re-layouts, on_device(): jnp.where(hits[:, None, :, slot, :, None], by_row[:, :, :, slot, None, :]...  10.1 us
    pallas_call x1, Pallas kernels, row_gather(): pl.pallas_call(row_gather_kernel, out_shape=jax.ShapeDtypeStruct((2 * cou...  7.16 us
  transfers between devices with their start and end apart: 1, of which 1 were waited for; matrix products, arithmetic and copies ran while one was open for 23% of the time, Pallas kernels for 0%

profile of v4, /device:TPU:1, one launch (start us, length us, event | category | flops | bytes accessed | tf_op | source)
XLA Modules:
  0.0 246.7 jit_solution(9780643913477076715)
XLA Ops:
  6.5 0.0 copy-start
  6.5 0.0 all-gather.2.cloned.1.call-start
  6.5 17.0 %shard_map.82 = bf16[768,512]{1,0:T(8,128)(2,1)} custom-call(bf16[96,512]{1,0:T(8,128)(2,1)} %x_ref.1), custom_call_target="tpu_custom_call" | custom-call | tf_op jit(solution)/shard_map/pallas_call | solution.py:84
  23.5 0.0 all-gather.2.cloned.1.call-update
  23.6 0.8 iota_compare_fusion
  24.3 0.1 copy.28
  24.4 0.7 fusion.8
  25.1 0.1 copy.29
  25.3 0.1 copy.31
  25.4 4.2 %slice_bitcast_fusion.1 = (bf16[3,128,32,128]{3,1,2,0:T(8,128)(2,1)S(1)}, bf16[3,128,32,128]{3,1,2,0:T(8,128)(2,1)S(1)}) fusion(bf16[3,128,32,2,128]{4,1,3,2,0:T(8,128)(2,1)} %bitcast.26), kind=kLoop, calls=%fused_computation.3 | loop fusion | bytes 12582912 | tf_op jit(solution)/shard_map/jit(_where)/broadcast_in_dim | solution.py:127
  29.6 2.0 copy.30
  31.6 3.6 %copy.32 = bf16[3,128,32,128]{3,2,1,0:T(8,128)(2,1)} copy(bf16[3,128,32,128]{3,1,2,0:T(8,128)(2,1)S(1)} %get-tuple-element.6) | data formatting | bytes 6291456 | tf_op jit(solution)/shard_map/jit(_where)/broadcast_in_dim | solution.py:127
  35.3 10.4 %select_select_fusion = bf16[3,128,32,6,128]{4,3,2,1,0:T(8,128)(2,1)} fusion(pred[3,32,6]{2,1,0:T(8,128)(4,1)S(1)} %copy.31, pred[3,32,6]{2,1,0:T(8,128)(4,1)S(1)} %copy.29, bf16[3,128,32,128]{3,2,1,0:T(8,128)(2,1)} %copy.32, bf16[3,128,32,128]{3,2,1,0:T(8,128)(2,1)S(1)} %copy.30), kind=kLoop, calls=%fused_computation | loop fusion | flops 18874368 | bytes 25166976 | tf_op jit(solution)/shard_map/jit(_where)/select_n | solution.py:127
  45.7 0.0 copy-start.2
  45.7 30.8 %select_n.32 = bf16[384,24576]{1,0:T(8,128)(2,1)} reshape(bf16[3,128,32,6,128]{4,3,2,1,0:T(8,128)(2,1)} %select_select_fusion) | data formatting | bytes 37748736 | tf_op jit(solution)/shard_map/jit(_where)/select_n | solution.py:127
  76.5 4.6 %convert_reduce_fusion = f32[3,32,2,128]{3,2,1,0:T(2,128)S(1)} fusion(bf16[3,32,2,128,128]{4,3,2,1,0:T(8,128)(2,1)} %param.9), kind=kLoop, calls=%fused_computation.1 | loop fusion | flops 6266880 | bytes 6389760 | tf_op jit(solution)/shard_map/reduce_sum | solution.py:117
  81.1 0.2 select_reduce_fusion
  81.3 0.0 copy-done.2
  81.3 126.4 %all-gather.2.cloned.1.call-done.table_ref = bf16[24576,512]{1,0:T(8,128)(2,1)} async-done(((bf16[768,512]{1,0:T(8,128)(2,1)}), bf16[24576,512]{1,0:T(8,128)(2,1)}) %all-gather.2.cloned.1.call-update) | async-done | bytes 25165840 | tf_op jit(solution)/shard_map/all_gather | solution.py:108
  207.7 7.2 %shard_map.83 = bf16[768,512]{1,0:T(8,128)(2,1)} custom-call(s32[384]{0:T(512)} %ids_ref.1, bf16[24576,512]{1,0:T(8,128)(2,1)} %all-gather.2.cloned.1.call-done.table_ref), custom_call_target="tpu_custom_call" | custom-call | tf_op jit(solution)/shard_map/pallas_call | solution.py:68
  214.9 2.2 reshape.31
  217.0 1.1 fusion.11
  218.1 0.0 copy-done
  218.1 0.4 fusion.5
  218.6 0.0 copy-start.1
  218.6 0.0 copy-start.3
  218.6 20.1 %fusion.3 = bf16[384,512]{1,0:T(8,128)(2,1)S(1)} fusion(bf16[384,24576]{1,0:T(8,128)(2,1)} %select_n.32, bf16[24576,512]{1,0:T(8,128)(2,1)} %all-gather.2.cloned.1.call-done.table_ref, f32[384]{0:T(512)S(1)} %sqrt_bitcast_fusion), kind=kOutput, calls=%fused_computation.9 | convolution fusion | flops 9664069632 | bytes 44434944 | tf_op jit(solution)/shard_map/dot_general | solution.py:132
  238.7 0.0 copy-done.1
  238.7 0.0 copy-done.3
  238.7 1.1 fusion.2
  (3 shorter events, 0.0 us)
Async XLA Ops:
  6.5 211.6 %copy-start = (bf16[512,512]{1,0:T(8,128)(2,1)S(1)}, bf16[512,512]{1,0:T(8,128)(2,1)}, u32[]{:S(2)}) copy-start(bf16[512,512]{1,0:T(8,128)(2,1)} %param.13) | copy-start | bytes 1572868
  6.5 201.2 %all-gather.2.cloned.1.call-start = ((), (), s32[]{:S(2)}) async-start(), calls=%async_computation | async-start | bytes 25952256 | tf_op jit(solution)/shard_map/all_gather | solution.py:108
  45.7 35.6 %copy-start.2 = (s32[384]{0:T(512)S(1)}, s32[384]{0:T(512)}, u32[]{:S(2)}) copy-start(s32[384]{0:T(512)} %ids_ref.1) | copy-start | bytes 4612
  218.6 20.1 %copy-start.1 = (bf16[512,512]{1,0:T(8,128)(2,1)S(1)}, bf16[512,512]{1,0:T(8,128)(2,1)}, u32[]{:S(2)}) copy-start(bf16[512,512]{1,0:T(8,128)(2,1)} %param.14) | copy-start | bytes 1572868
  218.6 20.1 %copy-start.3 = (f32[512]{0:T(512)S(1)}, f32[512]{0:T(512)}, u32[]{:S(2)}) copy-start(f32[512]{0:T(512)} %param.15) | copy-start | bytes 6148
Sparse Core Ops, SparseCore 0:
  23.7 183.9 all-gather.1

commit v5 on v2

--- a/solution.py
+++ b/solution.py
@@ -45,6 +45,66 @@
         arriving.wait_recv()
     for copy in sends:
         copy.wait_send()
+
+
+def product_kernel(ids_ref, a_ref, f_ref, table_ref, tot_ref, pairs_ref, sem):
+    step = pl.program_id(0)
+    count = ids_ref.shape[0]
+    last = table_ref.shape[0] - 1
+
+    def issue(r, carry):
+        row = jnp.minimum(jnp.maximum(ids_ref[r], 0), last)
+        start = pl.multiple_of((row // 2) * 2, 2)
+        pltpu.make_async_copy(
+            table_ref.at[pl.ds(start, 2)], pairs_ref.at[pl.ds(pl.multiple_of(r * 2, 2), 2)], sem
+        ).start()
+        return carry
+
+    @pl.when(step == 0)
+    def _():
+        tot_ref[...] = jnp.zeros_like(tot_ref)
+        lax.fori_loop(0, count, issue, 0, unroll=16)
+
+    tot_ref[...] += jnp.dot(a_ref[...], f_ref[...], preferred_element_type=jnp.float32)
+
+    @pl.when(step == pl.num_programs(0) - 1)
+    def _():
+        pltpu.make_async_copy(table_ref.at[pl.ds(0, 2 * count)], pairs_ref, sem).wait()
+
+
+def product_and_rows(dense, table, ids, depth=2048):
+    rows, inner = dense.shape
+    count, width = ids.shape[0], table.shape[1]
+    totals, pairs = pl.pallas_call(
+        product_kernel,
+        out_shape=(
+            jax.ShapeDtypeStruct((rows, width), jnp.float32),
+            jax.ShapeDtypeStruct((2 * count, width), table.dtype),
+        ),
+        grid_spec=pltpu.PrefetchScalarGridSpec(
+            num_scalar_prefetch=1,
+            grid=(inner // depth,),
+            in_specs=[
+                pl.BlockSpec((rows, depth), lambda k, ids: (0, k)),
+                pl.BlockSpec((depth, width), lambda k, ids: (k, 0)),
+                pl.BlockSpec(memory_space=pl.ANY),
+            ],
+            out_specs=[
+                pl.BlockSpec((rows, width), lambda k, ids: (0, 0)),
+                pl.BlockSpec((2 * count, width), lambda k, ids: (0, 0)),
+            ],
+            scratch_shapes=[pltpu.SemaphoreType.DMA(())],
+        ),
+        compiler_params=pltpu.CompilerParams(dimension_semantics=("arbitrary",)),
+        cost_estimate=pl.CostEstimate(
+            flops=2 * rows * inner * width,
+            bytes_accessed=2 * (rows * inner + inner * width),
+            transcendentals=0,
+        ),
+    )(ids, dense, table, table)
+    pairs = pairs.reshape(count, 2, width)
+    odd = (ids % 2 == 1)[:, None]
+    return totals, jnp.where(odd, pairs[:, 1, :], pairs[:, 0, :])
 
 
 def rep_gather(x, count):
@@ -97,8 +157,7 @@
         )
     dense = dense.reshape(local_rows, total_rows)
 
-    totals = jnp.dot(dense, everything, preferred_element_type=jnp.float32)
-    own_rows = jnp.take(everything, state_ids, axis=0)
+    totals, own_rows = product_and_rows(dense, everything, state_ids)
     neighbour = (totals / jnp.sqrt(degree)[:, None]).astype(jnp.bfloat16)
     activation = jnp.dot(own_rows, self_weight, preferred_element_type=jnp.float32)
     activation = activation + jnp.dot(

time: 251 us -> 249 us (level)
  Pallas kernels: 17 us -> 44.2 us
  matrix products: 21.9 us -> 2.72 us
  local copies, waits for them, and re-layouts: 54.5 us -> 44.7 us
    pallas_call x0 -> x1, Pallas kernels: none -> 27.2 us  [product_and_rows(): pl.pallas_call(product_kernel, out_shape=(jax.ShapeDtypeStruct((rows, wid...]
    dot_general x1 -> x0, matrix products: 20.3 us -> none  [on_device(): totals = jnp.dot(dense, everything, preferred_element_type=jnp.float32)]
    gather x1 -> x0, local copies, waits for them, and re-layouts: 13.5 us -> none  [on_device(): own_rows = jnp.take(everything, state_ids, axis=0)]
    broadcast_in_dim x6 -> x4, local copies, waits for them, and re-layouts: 10.1 us -> 9.9 us  [on_device(): jnp.where(hits[:, None, :, slot, :, None], by_row[:, :, :, slot, None, :]...]
where the time goes in v5:
time: 249 us; the launch traced here: 248 us
  waiting for transfers between devices  126 us (51%)
  local copies, waits for them, and re-layouts  44.7 us (18%)
  Pallas kernels  44.2 us (18%)
  other arithmetic  16.3 us (7%)
  between operations  13.5 us (5%)
  matrix products  2.72 us (1%)
    all_gather x1, waiting for transfers between devices, on_device(): everything = lax.all_gather(panels, 'grp', axis=0, tiled=True)  126 us
    select_n x1, local copies, waits for them, and re-layouts, on_device(): jnp.where(hits[:, None, :, slot, :, None], by_row[:, :, :, slot, None, :]...  30.8 us
    pallas_call x1, Pallas kernels, product_and_rows(): pl.pallas_call(product_kernel, out_shape=(jax.ShapeDtypeStruct((rows, wid...  27.2 us
    pallas_call x1, Pallas kernels, rep_gather(): pl.pallas_call(functools.partial(rep_gather_kernel, count), out_shape=jax...  17 us
    select_n x1, other arithmetic, on_device(): jnp.where(hits[:, None, :, slot, :, None], by_row[:, :, :, slot, None, :]...  10.6 us
    broadcast_in_dim x4, local copies, waits for them, and re-layouts, on_device(): jnp.where(hits[:, None, :, slot, :, None], by_row[:, :, :, slot, None, :]...  9.9 us
  transfers between devices with their start and end apart: 1, of which 1 were waited for; matrix products, arithmetic and copies ran while one was open for 23% of the time, Pallas kernels for 0%

profile of v5, /device:TPU:1, one launch (start us, length us, event | category | flops | bytes accessed | tf_op | source)
XLA Modules:
  0.0 247.8 jit_solution(16997155647963950395)
XLA Ops:
  6.5 0.0 copy-start
  6.5 0.0 all-gather.2.cloned.1.call-start
  6.5 17.0 %shard_map.82 = bf16[768,512]{1,0:T(8,128)(2,1)} custom-call(bf16[96,512]{1,0:T(8,128)(2,1)} %x_ref.1), custom_call_target="tpu_custom_call" | custom-call | tf_op jit(solution)/shard_map/pallas_call | solution.py:112
  23.5 0.0 all-gather.2.cloned.1.call-update
  23.6 0.8 iota_compare_fusion.1
  24.3 0.1 copy.27
  24.4 0.7 copy.26
  25.1 4.2 %slice_bitcast_fusion.1 = (bf16[3,128,32,128]{3,1,2,0:T(8,128)(2,1)S(1)}, bf16[3,128,32,128]{3,1,2,0:T(8,128)(2,1)S(1)}) fusion(bf16[3,128,32,2,128]{4,1,3,2,0:T(8,128)(2,1)} %bitcast.23), kind=kLoop, calls=%fused_computation.3 | loop fusion | bytes 12582912 | tf_op jit(solution)/shard_map/jit(_where)/broadcast_in_dim | solution.py:155
  29.4 2.0 copy.28
  31.4 3.7 %copy.29 = bf16[3,128,32,128]{3,2,1,0:T(8,128)(2,1)} copy(bf16[3,128,32,128]{3,1,2,0:T(8,128)(2,1)S(1)} %get-tuple-element.10) | data formatting | bytes 6291456 | tf_op jit(solution)/shard_map/jit(_where)/broadcast_in_dim | solution.py:155
  35.0 0.1 fusion.8
  35.2 10.6 %select_select_fusion = bf16[3,128,32,6,128]{4,3,2,1,0:T(8,128)(2,1)} fusion(pred[3,32,6]{2,1,0:T(8,128)(4,1)S(1)} %get-tuple-element.14, pred[3,32,6]{2,1,0:T(8,128)(4,1)S(1)} %get-tuple-element.13, bf16[3,128,32,128]{3,2,1,0:T(8,128)(2,1)} %copy.29, bf16[3,128,32,128]{3,2,1,0:T(8,128)(2,1)S(1)} %copy.28), kind=kLoop, calls=%fused_computation | loop fusion | flops 18874368 | bytes 25166976 | tf_op jit(solution)/shard_map/jit(_where)/select_n | solution.py:155
  45.8 0.0 copy-start.1
  45.8 30.8 %select_n.31.a_ref = bf16[384,24576]{1,0:T(8,128)(2,1)} reshape(bf16[3,128,32,6,128]{4,3,2,1,0:T(8,128)(2,1)} %select_select_fusion) | data formatting | bytes 37748736 | tf_op jit(solution)/shard_map/jit(_where)/select_n | solution.py:155
  76.6 4.6 %convert_reduce_fusion = f32[3,32,2,128]{3,2,1,0:T(2,128)S(1)} fusion(bf16[3,32,2,128,128]{4,3,2,1,0:T(8,128)(2,1)} %param.9), kind=kLoop, calls=%fused_computation.1 | loop fusion | flops 6266880 | bytes 6389760 | tf_op jit(solution)/shard_map/reduce_sum | solution.py:145
  81.1 0.2 select_reduce_fusion
  81.3 0.0 copy-done.1
  81.4 0.0 copy-start.2
  81.4 0.0 copy-start.3
  81.4 126.3 %all-gather.2.cloned.1.call-done.f_ref.table_ref = bf16[24576,512]{1,0:T(8,128)(2,1)} async-done(((bf16[768,512]{1,0:T(8,128)(2,1)}), bf16[24576,512]{1,0:T(8,128)(2,1)}) %all-gather.2.cloned.1.call-update) | async-done | bytes 25165840 | tf_op jit(solution)/shard_map/all_gather | solution.py:136
  207.7 27.2 %shard_map.83 = (f32[384,512]{1,0:T(8,128)}, bf16[768,512]{1,0:T(8,128)(2,1)}) custom-call(s32[384]{0:T(512)} %ids_ref.1, bf16[384,24576]{1,0:T(8,128)(2,1)} %select_n.31.a_ref, bf16[24576,512]{1,0:T(8,128)(2,1)} %all-gather.2.cloned.1.call-done.f_ref.table_ref, bf16[24576,512]{1,0:T(8,128)(2,1)} %all-gather.2.cloned.1.call-done.f_ref.table_ref), custom_call_target="tpu_custom_call" | custom-call | flops 9663676416 | bytes 44040192 | tf_op jit(solution)/shard_map/pallas_call | solution.py:78
  234.9 2.2 reshape.31
  237.1 1.1 fusion.11
  238.2 0.0 copy-done
  238.2 0.4 fusion.4
  238.6 0.0 copy-done.2
  238.6 0.0 copy-done.3
  238.6 2.3 fusion.2
  (3 shorter events, 0.0 us)
Async XLA Ops:
  6.5 231.6 %copy-start = (bf16[512,512]{1,0:T(8,128)(2,1)S(1)}, bf16[512,512]{1,0:T(8,128)(2,1)}, u32[]{:S(2)}) copy-start(bf16[512,512]{1,0:T(8,128)(2,1)} %param.13) | copy-start | bytes 1572868
  6.5 201.2 %all-gather.2.cloned.1.call-start = ((), (), s32[]{:S(2)}) async-start(), calls=%async_computation | async-start | bytes 25952256 | tf_op jit(solution)/shard_map/all_gather | solution.py:136
  45.8 35.5 %copy-start.1 = (s32[384]{0:T(512)S(1)}, s32[384]{0:T(512)}, u32[]{:S(2)}) copy-start(s32[384]{0:T(512)} %ids_ref.1) | copy-start | bytes 4612
  81.4 157.2 %copy-start.2 = (bf16[512,512]{1,0:T(8,128)(2,1)S(1)}, bf16[512,512]{1,0:T(8,128)(2,1)}, u32[]{:S(2)}) copy-start(bf16[512,512]{1,0:T(8,128)(2,1)} %param.14) | copy-start | bytes 1572868
  81.4 157.2 %copy-start.3 = (f32[512]{0:T(512)S(1)}, f32[512]{0:T(512)}, u32[]{:S(2)}) copy-start(f32[512]{0:T(512)} %param.15) | copy-start | bytes 6148
Sparse Core Ops, SparseCore 0:
  23.7 183.9 all-gather.1

commit v6 on v4

--- a/solution.py
+++ b/solution.py
@@ -74,9 +74,10 @@
         ],
         out_specs=pl.BlockSpec(memory_space=pltpu.VMEM),
         scratch_shapes=[pltpu.SemaphoreType.DMA(())],
-    )(ids, table).reshape(count, 2, width)
-    odd = (ids % 2 == 1)[:, None]
-    return jnp.where(odd, pairs[:, 1, :], pairs[:, 0, :])
+    )(ids, table)
+    wanted = 2 * lax.broadcasted_iota(jnp.int32, (count, 1), 0) + (ids % 2)[:, None]
+    picks = (lax.broadcasted_iota(jnp.int32, (count, 2 * count), 1) == wanted).astype(table.dtype)
+    return jnp.dot(picks, pairs, preferred_element_type=jnp.float32).astype(table.dtype)
 
 
 def rep_gather(x, count):

time: 248 us -> 246 us (level)
  local copies, waits for them, and re-layouts: 44.3 us -> 41 us
  transfers between devices with their start and end apart: 1 -> 1, of which waited for: 1 -> 1; matrix products, arithmetic and copies ran while one was open for 23% -> 24% of each run, Pallas kernels for 0% -> 0%
where the time goes in v6:
time: 246 us; the launch traced here: 245 us
  waiting for transfers between devices  126 us (51%)
  local copies, waits for them, and re-layouts  41 us (17%)
  Pallas kernels  24.1 us (10%)
  matrix products  23.1 us (9%)
  other arithmetic  16.7 us (7%)
  between operations  13.5 us (5%)
    all_gather x1, waiting for transfers between devices, on_device(): everything = lax.all_gather(panels, 'grp', axis=0, tiled=True)  126 us
    select_n x1, local copies, waits for them, and re-layouts, on_device(): jnp.where(hits[:, None, :, slot, :, None], by_row[:, :, :, slot, None, :]...  30.8 us
    dot_general x1, matrix products, on_device(): totals = jnp.dot(dense, everything, preferred_element_type=jnp.float32)  20.1 us
    pallas_call x1, Pallas kernels, rep_gather(): pl.pallas_call(functools.partial(rep_gather_kernel, count), out_shape=jax...  17 us
    select_n x1, other arithmetic, on_device(): jnp.where(hits[:, None, :, slot, :, None], by_row[:, :, :, slot, None, :]...  10.4 us
    broadcast_in_dim x6, local copies, waits for them, and re-layouts, on_device(): jnp.where(hits[:, None, :, slot, :, None], by_row[:, :, :, slot, None, :]...  10.1 us
    pallas_call x1, Pallas kernels, row_gather(): pl.pallas_call(row_gather_kernel, out_shape=jax.ShapeDtypeStruct((2 * cou...  7.16 us
  transfers between devices with their start and end apart: 1, of which 1 were waited for; matrix products, arithmetic and copies ran while one was open for 24% of the time, Pallas kernels for 0%

profile of v6, /device:TPU:1, one launch (start us, length us, event | category | flops | bytes accessed | tf_op | source)
XLA Modules:
  0.0 244.9 jit_solution(9209989980477042124)
XLA Ops:
  6.5 0.0 copy-start
  6.5 0.0 all-gather.2.cloned.1.call-start
  6.5 17.0 %shard_map.82 = bf16[768,512]{1,0:T(8,128)(2,1)} custom-call(bf16[96,512]{1,0:T(8,128)(2,1)} %x_ref.1), custom_call_target="tpu_custom_call" | custom-call | tf_op jit(solution)/shard_map/pallas_call | solution.py:85
  23.5 0.0 all-gather.2.cloned.1.call-update
  23.6 0.8 iota_compare_fusion.3
  24.3 0.1 copy.21
  24.4 0.7 fusion.7
  25.1 0.1 copy.22
  25.3 0.1 copy.24
  25.4 4.2 %slice_bitcast_fusion.1 = (bf16[3,128,32,128]{3,1,2,0:T(8,128)(2,1)S(1)}, bf16[3,128,32,128]{3,1,2,0:T(8,128)(2,1)S(1)}) fusion(bf16[3,128,32,2,128]{4,1,3,2,0:T(8,128)(2,1)} %bitcast.17), kind=kLoop, calls=%fused_computation.3 | loop fusion | bytes 12582912 | tf_op jit(solution)/shard_map/jit(_where)/broadcast_in_dim | solution.py:128
  29.6 2.0 copy.23
  31.6 3.6 %copy.25 = bf16[3,128,32,128]{3,2,1,0:T(8,128)(2,1)} copy(bf16[3,128,32,128]{3,1,2,0:T(8,128)(2,1)S(1)} %get-tuple-element.6) | data formatting | bytes 6291456 | tf_op jit(solution)/shard_map/jit(_where)/broadcast_in_dim | solution.py:128
  35.3 10.4 %select_select_fusion = bf16[3,128,32,6,128]{4,3,2,1,0:T(8,128)(2,1)} fusion(pred[3,32,6]{2,1,0:T(8,128)(4,1)S(1)} %copy.24, pred[3,32,6]{2,1,0:T(8,128)(4,1)S(1)} %copy.22, bf16[3,128,32,128]{3,2,1,0:T(8,128)(2,1)} %copy.25, bf16[3,128,32,128]{3,2,1,0:T(8,128)(2,1)S(1)} %copy.23), kind=kLoop, calls=%fused_computation | loop fusion | flops 18874368 | bytes 25166976 | tf_op jit(solution)/shard_map/jit(_where)/select_n | solution.py:128
  45.7 0.0 copy-start.2
  45.7 30.8 %select_n.27 = bf16[384,24576]{1,0:T(8,128)(2,1)} reshape(bf16[3,128,32,6,128]{4,3,2,1,0:T(8,128)(2,1)} %select_select_fusion) | data formatting | bytes 37748736 | tf_op jit(solution)/shard_map/jit(_where)/select_n | solution.py:128
  76.5 4.6 %convert_reduce_fusion = f32[3,32,2,128]{3,2,1,0:T(2,128)S(1)} fusion(bf16[3,32,2,128,128]{4,3,2,1,0:T(8,128)(2,1)} %param.9), kind=kLoop, calls=%fused_computation.1 | loop fusion | flops 6266880 | bytes 6389760 | tf_op jit(solution)/shard_map/reduce_sum | solution.py:118
  81.1 0.2 select_reduce_fusion
  81.3 0.0 copy-done.2
  81.3 126.4 %all-gather.2.cloned.1.call-done.table_ref = bf16[24576,512]{1,0:T(8,128)(2,1)} async-done(((bf16[768,512]{1,0:T(8,128)(2,1)}), bf16[24576,512]{1,0:T(8,128)(2,1)}) %all-gather.2.cloned.1.call-update) | async-done | bytes 25165840 | tf_op jit(solution)/shard_map/all_gather | solution.py:109
  207.7 7.2 %shard_map.83 = bf16[768,512]{1,0:T(8,128)(2,1)} custom-call(s32[384]{0:T(512)} %ids_ref.1, bf16[24576,512]{1,0:T(8,128)(2,1)} %all-gather.2.cloned.1.call-done.table_ref), custom_call_target="tpu_custom_call" | custom-call | tf_op jit(solution)/shard_map/pallas_call | solution.py:68
  214.9 0.0 copy-done
  214.9 1.9 fusion.4
  216.8 0.0 copy-start.1
  216.8 0.0 copy-start.3
  216.8 20.1 %fusion.3 = bf16[384,512]{1,0:T(8,128)(2,1)S(1)} fusion(bf16[384,24576]{1,0:T(8,128)(2,1)} %select_n.27, bf16[24576,512]{1,0:T(8,128)(2,1)} %all-gather.2.cloned.1.call-done.table_ref, f32[384]{0:T(512)S(1)} %sqrt_bitcast_fusion), kind=kOutput, calls=%fused_computation.10 | convolution fusion | flops 9664069632 | bytes 44434944 | tf_op jit(solution)/shard_map/dot_general | solution.py:133
  236.9 0.0 copy-done.1
  236.9 0.0 copy-done.3
  236.9 1.1 fusion.2
  (3 shorter events, 0.0 us)
Async XLA Ops:
  6.5 208.3 %copy-start = (bf16[512,512]{1,0:T(8,128)(2,1)S(1)}, bf16[512,512]{1,0:T(8,128)(2,1)}, u32[]{:S(2)}) copy-start(bf16[512,512]{1,0:T(8,128)(2,1)} %param.13) | copy-start | bytes 1572868
  6.5 201.2 %all-gather.2.cloned.1.call-start = ((), (), s32[]{:S(2)}) async-start(), calls=%async_computation | async-start | bytes 25952256 | tf_op jit(solution)/shard_map/all_gather | solution.py:109
  45.7 35.5 %copy-start.2 = (s32[384]{0:T(512)S(1)}, s32[384]{0:T(512)}, u32[]{:S(2)}) copy-start(s32[384]{0:T(512)} %ids_ref.1) | copy-start | bytes 4612
  216.8 20.1 %copy-start.1 = (bf16[512,512]{1,0:T(8,128)(2,1)S(1)}, bf16[512,512]{1,0:T(8,128)(2,1)}, u32[]{:S(2)}) copy-start(bf16[512,512]{1,0:T(8,128)(2,1)} %param.14) | copy-start | bytes 1572868
  216.8 20.1 %copy-start.3 = (f32[512]{0:T(512)S(1)}, f32[512]{0:T(512)}, u32[]{:S(2)}) copy-start(f32[512]{0:T(512)} %param.15) | copy-start | bytes 6148
Sparse Core Ops, SparseCore 0:
  23.7 183.9 all-gather.1
